TPU v7x, 32 devices: a whole 2x2x4 slice. The times are simulated.
32 devices in a mesh: grp: 4 (over y, x), pos: 8 (over z, core).
Axes of the slice: x: 2, y: 2, z: 4, core: 2. Of those that a mesh axis runs over, the one named last changes fastest.
Arguments:
- tiles: float32 [4, 8, 12, 256, 256], P('grp', 'pos'), may hold values from -0.109375 to 0.109375
- tile_row: int32 [4, 8, 12], P('grp', 'pos'), may hold values from 0 to 7
- tile_col: int32 [4, 8, 12], P('grp', 'pos'), may hold values from 0 to 7
- tile_count: int32 [4, 8], P('grp', 'pos'), may hold values from 1 to 12, as said below
- energies: float32 [16384], P('pos'), may hold values from 1 to 10
- basis: float32 [16, 16384], P(None, 'pos'), may hold values from -6 to 6
- prev_basis: float32 [16, 16384], P(None, 'pos'), may hold values from -6 to 6
- beta_prev: float32 [16, 16], replicated, may hold values from -3 to 3
Outputs:
- next_basis: float32 [16, 16384], P(None, 'pos')
- alpha: float32 [16, 16], replicated
- beta: float32 [16, 16], replicated
Inputs may be any that keep to these rules, and one draw needn't show every extreme that they name: `tile_count`: some segment of some diagonal uses all 12 slots in every draw.
All inputs are finite; a program needn't handle non-finite values.
Results may differ from a plain program's by a relative error of at most 0.00021.
Values sent between devices are 32-bit elements; how exact they have to be, the bound alone decides.
A program may use at most 64 MiB of HBM per device.

v0:
```python
import jax
import jax.numpy as jnp
from jax import lax
from jax.sharding import PartitionSpec as P


def passed_along(array, axis, by):
    peers = lax.axis_size(axis)
    return lax.ppermute(array, axis, [(i, (i + by) % peers) for i in range(peers)])


def matmul(left, right):
    return jnp.dot(left, right, precision=lax.Precision.HIGHEST)


def product(left, right):
    return jnp.dot(left, right.T, precision=lax.Precision.HIGHEST)


def rotate(values_in, offset):
    return passed_along(values_in, "pos", offset)


def shards(tiles, tile_row, tile_col, tile_count, energies, basis, prev_basis, beta_prev):
    slot_count = tiles.shape[2]
    tile_width = tiles.shape[-1]
    blocks = tiles.reshape(slot_count, tile_width, tile_width)
    vector_count, seg_len = basis.shape
    per_side = seg_len // tile_width
    highest = lax.Precision.HIGHEST
    live_mask = (jnp.arange(slot_count, dtype=jnp.int32) < tile_count.reshape(())).astype(
        jnp.float32
    )
    sides = jnp.arange(per_side, dtype=jnp.int32)
    row_hot = (tile_row.reshape(slot_count)[:, None] == sides[None, :]).astype(
        jnp.float32
    ) * live_mask[:, None]
    col_hot = (tile_col.reshape(slot_count)[:, None] == sides[None, :]).astype(
        jnp.float32
    ) * live_mask[:, None]
    own_rows = basis.reshape(vector_count, per_side, tile_width)
    group_index = lax.axis_index("grp")
    bit_count = lax.axis_size("grp").bit_length() - 1
    seg_total = lax.axis_size("pos")
    total_rows = float(seg_len * seg_total)

    def pick(level, arrived, kept):
        return jnp.where(group_index // (1 << level) % 2 == 1, arrived, kept)

    far_rows = own_rows
    for level in range(bit_count):
        far_rows = pick(level, rotate(far_rows, -(1 << level)), far_rows)
    picked = jnp.einsum("kt,btj->kbj", col_hot, far_rows, precision=highest)
    parts = jnp.einsum("kbj,kij->kbi", picked, blocks, precision=highest)
    forward = jnp.einsum("kt,kbi->bti", row_hot, parts, precision=highest)
    picked = jnp.einsum("kt,bti->kbi", row_hot, own_rows, precision=highest)
    parts = jnp.einsum("kbi,kij->kbj", picked, blocks, precision=highest)
    back_rows = jnp.einsum("kt,kbj->btj", col_hot, parts, precision=highest)
    for level in range(bit_count):
        back_rows = pick(level, rotate(back_rows, 1 << level), back_rows)
    partial_sum = (forward + back_rows).reshape(vector_count, seg_len)
    applied = lax.psum(partial_sum, "grp") + energies[None, :] * basis
    alpha = lax.psum(product(basis, applied), "pos") / total_rows
    residual = applied - matmul(alpha.T, basis) - matmul(beta_prev, prev_basis)
    gram = lax.psum(product(residual, residual), "pos") / total_rows
    factor = jnp.linalg.cholesky(gram)
    next_rows = jax.scipy.linalg.solve_triangular(factor, residual, lower=True)
    return (next_rows, alpha, factor)


def solution(mesh):
    in_specs = (
        P("grp", "pos", None, None, None),
        P("grp", "pos", None),
        P("grp", "pos", None),
        P("grp", "pos"),
        P("pos"),
        P(None, "pos"),
        P(None, "pos"),
        P(),
    )
    out_specs = (P(None, "pos"), P(), P())
    return jax.shard_map(shards, mesh=mesh, in_specs=in_specs, out_specs=out_specs, check_vma=False)
```

profile of v0, /device:TPU:0, one launch (start us, length us, event | category | flops | bytes accessed | tf_op | source)
XLA Modules:
  0.0 120.1 jit_solution(79853631742649549)
XLA Ops:
  7.2 0.0 copy-start
  7.2 0.0 copy-start.5
  7.2 0.0 all-reduce.2.cloned.1.call-start
  7.2 1.1 copy.19
  8.3 4.6 %collective-permute-start = (f32[16,8,256]{2,1,0:T(8,128)S(1)}, f32[16,8,256]{2,1,0:T(8,128)}, u32[]{:S(2)}, u32[]{:S(2)}) collective-permute-start(f32[16,8,256]{2,1,0:T(8,128)S(1)} %bitcast.48), channel_id=1, source_target_pairs={{0,7},{1,0},{2,1},{3,2},{4,3},{5,4},{6,5},{7,6},{8,15},{9,8},{10,9... | collective-permute-start | bytes 393224 | tf_op jit(solution)/shard_map/ppermute | solution.py:9
  13.6 1.1 fusion.15
  14.7 0.0 copy-done
  14.7 1.7 %fusion = f32[12,16,256]{2,1,0:T(8,128)S(1)} fusion(f32[1,1,12,256,256]{4,3,2,1,0:T(8,128)S(1)} %copy-done, f32[12,16,256]{2,0,1:T(8,128)S(1)} %fusion.15), kind=kOutput, calls=%fused_computation | convolution fusion | flops 150994944 | bytes 3538944 | tf_op jit(solution)/shard_map/kbi,kij->kbj/dot_general | solution.py:57
  16.4 0.0 copy-done.5
  16.4 0.4 convolution_bitcast_fusion
  16.8 0.0 copy-start.1
  16.8 0.0 copy-start.3
  16.8 0.1 collective-permute-start.2
  16.9 0.0 collective-permute-done
  17.0 1.1 collective-permute-start.1
  18.0 5.2 %collective-permute-done.2 = f32[16,8,256]{2,1,0:T(8,128)} collective-permute-done((f32[16,8,256]{2,1,0:T(8,128)S(1)}, f32[16,8,256]{2,1,0:T(8,128)}, u32[]{:S(2)}, u32[]{:S(2)}) %collective-permute-start.2) | collective-permute-done | bytes 131104 | tf_op jit(solution)/shard_map/ppermute | solution.py:9
  23.3 0.0 copy-start.2
  23.3 0.0 copy-start.4
  23.3 0.1 collective-permute-start.3
  23.4 0.0 collective-permute-done.1
  23.4 0.4 fusion.8
  23.8 2.8 %fusion.2 = f32[12,16,256]{2,1,0:T(8,128)S(1)} fusion(f32[1,1,12,256,256]{4,3,2,1,0:T(8,128)S(1)} %copy-done, f32[12,16,256]{2,0,1:T(8,128)S(1)} %fusion.8), kind=kOutput, calls=%fused_computation.2 | convolution fusion | flops 150994944 | bytes 3538944 | tf_op jit(solution)/shard_map/kbj,kij->kbi/dot_general | solution.py:54
  26.6 1.1 convolution_bitcast_fusion.1
  27.7 2.5 %collective-permute-done.3 = f32[16,8,256]{2,1,0:T(8,128)S(1)} collective-permute-done((f32[16,8,256]{2,1,0:T(8,128)S(1)}, f32[16,8,256]{2,1,0:T(8,128)S(1)}, u32[]{:S(2)}, u32[]{:S(2)}) %collective-permute-start.3) | collective-permute-done | bytes 131104 | tf_op jit(solution)/shard_map/ppermute | solution.py:9
  30.2 0.7 copy.20
  30.9 0.0 all-reduce.2.cloned.1.call-update
  30.9 42.9 %all-reduce.2.cloned.1.call-done = f32[16,2048]{1,0:T(8,128)} async-done(((f32[16,2048]{1,0:T(8,128)}), f32[16,2048]{1,0:T(8,128)}) %all-reduce.2.cloned.1.call-update) | async-done | bytes 131088 | tf_op jit(solution)/shard_map/psum | solution.py:62
  73.9 0.0 copy-done.1
  73.9 0.0 copy-done.3
  73.9 1.2 convolution_bitcast_fusion.2
  75.0 16.2 %psum.22 = f32[16,16]{0,1:T(8,128)S(1)} all-reduce(f32[16,16]{0,1:T(8,128)S(1)} %convolution_bitcast_fusion.2), channel_id=1, replica_groups=mesh['grp'=4,'pos'=8] {'pos'}, use_global_device_ids=true, to_apply=%region_1.2 | all-reduce | flops 256 | bytes 2048 | tf_op jit(solution)/shard_map/psum | solution.py:63
  91.2 0.7 copy.13
  91.9 1.2 convolution_subtract_fusion.1
  93.1 0.0 copy-done.2
  93.1 0.0 copy-done.4
  93.1 0.3 convolution_subtract_fusion
  93.4 0.2 fusion.40
  93.6 14.0 %psum.23 = f32[16,16]{0,1:T(8,128)S(1)} all-reduce(f32[16,16]{0,1:T(8,128)S(1)} %fusion.40), channel_id=1, replica_groups=mesh['grp'=4,'pos'=8] {'pos'}, use_global_device_ids=true, to_apply=%region_2.3 | all-reduce | flops 256 | bytes 2048 | tf_op jit(solution)/shard_map/psum | solution.py:65
  107.6 0.1 copy.12
  107.7 1.5 %cholesky.16 = f32[16,16]{1,0:T(8,128)S(1)} custom-call(f32[16,16]{1,0:T(8,128)S(1)} %fusion.14), custom_call_target="Cholesky" | custom-call | tf_op jit(solution)/shard_map/jit(cholesky)/cholesky | solution.py:66
  109.1 0.6 compare_reduce_fusion
  109.8 1.2 %select_bitcast_fusion = (f32[1,16,16]{2,1,0:T(8,128)S(1)}, f32[16,16]{1,0:T(8,128)}) fusion(f32[16,16]{1,0:T(8,128)S(1)} %cholesky.16, pred[]{:T(512)} %compare_reduce_fusion), kind=kLoop, calls=%fused_computation.25 | loop fusion | flops 1024 | bytes 3073 | tf_op jit(solution)/shard_map/jit(_solve_triangular)/triangular_solve | solution.py:67
  111.0 1.2 %custom-call.7 = f32[1,16,16]{1,2,0:T(8,128)S(1)} custom-call(f32[1,16,16]{2,1,0:T(8,128)S(1)} %get-tuple-element.6), custom_call_target="InvertDiagBlocksLowerTriangular" | custom-call | tf_op jit(solution)/shard_map/jit(_solve_triangular)/triangular_solve | solution.py:67
  112.3 1.0 fusion.12
  (8 shorter events, 0.1 us)
Async XLA Ops:
  7.2 7.5 %copy-start = (f32[1,1,12,256,256]{4,3,2,1,0:T(8,128)S(1)}, f32[1,1,12,256,256]{4,3,2,1,0:T(8,128)}, u32[]{:S(2)}) copy-start(f32[1,1,12,256,256]{4,3,2,1,0:T(8,128)} %param.8) | copy-start | bytes 9437188
  7.2 9.2 %copy-start.5 = (s32[1,1,12]{2,1,0:T(1,128)S(1)}, s32[1,1,12]{2,1,0:T(1,128)}, u32[]{:S(2)}) copy-start(s32[1,1,12]{2,1,0:T(1,128)} %param.10) | copy-start | bytes 148
  7.2 66.7 %all-reduce.2.cloned.1.call-start = ((), (), s32[]{:S(2)}) async-start(), calls=%async_computation | async-start | bytes 262144 | tf_op jit(solution)/shard_map/psum | solution.py:62
  8.3 8.6 %collective-permute-start = (f32[16,8,256]{2,1,0:T(8,128)S(1)}, f32[16,8,256]{2,1,0:T(8,128)}, u32[]{:S(2)}, u32[]{:S(2)}) collective-permute-start(f32[16,8,256]{2,1,0:T(8,128)S(1)} %bitcast.48), channel_id=1, source_target_pairs={{0,7},{1,0},{2,1},{3,2},{4,3},{5,4},{6,5},{7,6},{8,15},{9,8},{10,9... | collective-permute-start | bytes 393224 | tf_op jit(solution)/shard_map/ppermute | solution.py:9
  16.8 57.0 %copy-start.1 = (f32[16,2048]{1,0:T(8,128)S(1)}, f32[16,2048]{1,0:T(8,128)}, u32[]{:S(2)}) copy-start(f32[16,2048]{1,0:T(8,128)} %param.13) | copy-start | bytes 393220
  16.8 57.0 %copy-start.3 = (f32[2048]{0:T(1024)S(1)}, f32[2048]{0:T(1024)}, u32[]{:S(2)}) copy-start(f32[2048]{0:T(1024)} %param.12) | copy-start | bytes 24580
  16.8 6.5 %collective-permute-start.2 = (f32[16,8,256]{2,1,0:T(8,128)S(1)}, f32[16,8,256]{2,1,0:T(8,128)}, u32[]{:S(2)}, u32[]{:S(2)}) collective-permute-start(f32[16,8,256]{2,1,0:T(8,128)S(1)} %convolution_bitcast_fusion), channel_id=1, source_target_pairs={{0,1},{1,2},{2,3},{3,4},{4,5},{5,6},{6,7},{7,0},{8,9},{9,10},{10,1... | collective-permute-start | bytes 393224 | tf_op jit(solution)/shard_map/ppermute | solution.py:9
  17.0 6.4 %collective-permute-start.1 = (f32[16,8,256]{2,1,0:T(8,128)S(1)}, f32[16,8,256]{2,1,0:T(8,128)S(1)}, u32[]{:S(2)}, u32[]{:S(2)}) collective-permute-start(f32[16,8,256]{2,1,0:T(8,128)S(1)} %broadcast_select_fusion.1), channel_id=1, source_target_pairs={{0,6},{1,7},{2,0},{3,1},{4,2},{5,3},{6,4},{7,5},{8,14},{9,15},{10,... | collective-permute-start | bytes 393224 | tf_op jit(solution)/shard_map/ppermute | solution.py:9
  23.3 69.8 %copy-start.2 = (f32[16,2048]{1,0:T(8,128)S(1)}, f32[16,2048]{1,0:T(8,128)}, u32[]{:S(2)}) copy-start(f32[16,2048]{1,0:T(8,128)} %param.14) | copy-start | bytes 393220
  23.3 69.8 %copy-start.4 = (f32[16,16]{1,0:T(8,128)S(1)}, f32[16,16]{1,0:T(8,128)}, u32[]{:S(2)}) copy-start(f32[16,16]{1,0:T(8,128)} %param.15) | copy-start | bytes 3076
  23.3 6.8 %collective-permute-start.3 = (f32[16,8,256]{2,1,0:T(8,128)S(1)}, f32[16,8,256]{2,1,0:T(8,128)S(1)}, u32[]{:S(2)}, u32[]{:S(2)}) collective-permute-start(f32[16,8,256]{2,1,0:T(8,128)S(1)} %broadcast_select_fusion), channel_id=1, source_target_pairs={{0,2},{1,3},{2,4},{3,5},{4,6},{5,7},{6,0},{7,1},{8,10},{9,11},{10,... | collective-permute-start | bytes 393224 | tf_op jit(solution)/shard_map/ppermute | solution.py:9
Sparse Core Ops, SparseCore 0:
  31.0 42.7 all-reduce.1
where the time goes:
time: 120 us
  waiting for transfers between devices  50.7 us (42%)
  blocking collectives  30.2 us (25%)
  between operations  14.9 us (12%)
  matrix products  11.3 us (9%)
  starting transfers between devices  5.78 us (5%)
  other arithmetic  4.7 us (4%)
  local copies, waits for them, and re-layouts  2.58 us (2%)
    psum x1, waiting for transfers between devices, shards(): applied = lax.psum(partial_sum, 'grp') + energies[None, :] * basis  42.9 us
    psum x1, blocking collectives, shards(): alpha = lax.psum(product(basis, applied), 'pos') / total_rows  16.2 us
    psum x1, blocking collectives, shards(): gram = lax.psum(product(residual, residual), 'pos') / total_rows  14 us
    ppermute x4, waiting for transfers between devices, passed_along(): lax.ppermute(array, axis, [(i, (i + by) % peers) for i in range(peers)])  7.71 us
    ppermute x4, starting transfers between devices, passed_along(): lax.ppermute(array, axis, [(i, (i + by) % peers) for i in range(peers)])  5.74 us
    dot_general x1, matrix products, shards(): parts = jnp.einsum('kbj,kij->kbi', picked, blocks, precision=highest)  2.76 us
    unnamed x15, local copies, waits for them, and re-layouts  2.51 us
    another operation x2, other arithmetic, shards(): next_rows = jax.scipy.linalg.solve_triangular(factor, residual, lower=True)  2.47 us
  transfers between devices with their start and end apart: 5, of which 3 were waited for; matrix products, arithmetic and copies ran while one was open for 6% of the time, Pallas kernels for 0%

commit v1 on v0

--- a/solution.py
+++ b/solution.py
@@ -2,6 +2,12 @@
 import jax.numpy as jnp
 from jax import lax
 from jax.sharding import PartitionSpec as P
+
+
+def summed_here(block, name):
+    parts = lax.all_gather(block, name, axis=0, tiled=False)
+    total = parts.sum(axis=0)
+    return total
 
 
 def passed_along(array, axis, by):
@@ -59,7 +65,7 @@
     for level in range(bit_count):
         back_rows = pick(level, rotate(back_rows, 1 << level), back_rows)
     partial_sum = (forward + back_rows).reshape(vector_count, seg_len)
-    applied = lax.psum(partial_sum, "grp") + energies[None, :] * basis
+    applied = summed_here(partial_sum, "grp") + energies[None, :] * basis
     alpha = lax.psum(product(basis, applied), "pos") / total_rows
     residual = applied - matmul(alpha.T, basis) - matmul(beta_prev, prev_basis)
     gram = lax.psum(product(residual, residual), "pos") / total_rows

time: 120 us -> 72.9 us (0.61)
  waiting for transfers between devices: 50.7 us -> 7.69 us
  between operations: 14.9 us -> 1.52 us
  blocking collectives: 30.2 us -> 39.6 us
    psum x1 -> x0, waiting for transfers between devices: 42.9 us -> none  [shards(): applied = lax.psum(partial_sum, 'grp') + energies[None, :] * basis]
    all_gather x0 -> x1, blocking collectives: none -> 11.7 us  [summed_here(): parts = lax.all_gather(block, name, axis=0, tiled=False)]
    psum x1, blocking collectives: 16.2 us -> 14 us  [shards(): alpha = lax.psum(product(basis, applied), 'pos') / total_rows]
    unnamed x15 -> x10, local copies, waits for them, and re-layouts: 2.51 us -> 1.8 us
  transfers between devices with their start and end apart: 5 -> 4, of which waited for: 3 -> 2; matrix products, arithmetic and copies ran while one was open for 6% -> 10% of each run, Pallas kernels for 0% -> 0%
where the time goes in v1:
time: 72.9 us; the launch traced here: 72.6 us
  blocking collectives  39.6 us (54%)
  matrix products  10.4 us (14%)
  waiting for transfers between devices  7.69 us (11%)
  other arithmetic  5.78 us (8%)
  starting transfers between devices  5.75 us (8%)
  local copies, waits for them, and re-layouts  1.89 us (3%)
  between operations  1.52 us (2%)
    psum x1, blocking collectives, shards(): alpha = lax.psum(product(basis, applied), 'pos') / total_rows  14 us
    psum x1, blocking collectives, shards(): gram = lax.psum(product(residual, residual), 'pos') / total_rows  14 us
    all_gather x1, blocking collectives, summed_here(): parts = lax.all_gather(block, name, axis=0, tiled=False)  11.7 us
    ppermute x4, waiting for transfers between devices, passed_along(): lax.ppermute(array, axis, [(i, (i + by) % peers) for i in range(peers)])  7.69 us
    ppermute x4, starting transfers between devices, passed_along(): lax.ppermute(array, axis, [(i, (i + by) % peers) for i in range(peers)])  5.75 us
    dot_general x1, matrix products, shards(): parts = jnp.einsum('kbj,kij->kbi', picked, blocks, precision=highest)  2.76 us
    another operation x2, other arithmetic, shards(): next_rows = jax.scipy.linalg.solve_triangular(factor, residual, lower=True)  2.47 us
    another operation x3, other arithmetic, shards(): factor = jnp.linalg.cholesky(gram)  2.13 us
  transfers between devices with their start and end apart: 4, of which 2 were waited for; matrix products, arithmetic and copies ran while one was open for 10% of the time, Pallas kernels for 0%

profile of v1, /device:TPU:0, one launch (start us, length us, event | category | flops | bytes accessed | tf_op | source)
XLA Modules:
  0.0 72.6 jit_solution(12245836137930768351)
XLA Ops:
  0.6 0.0 copy-start
  0.6 0.0 copy-start.3
  0.7 1.1 %copy.22 = f32[2,8,8,256]{3,2,1,0:T(8,128)S(1)} copy(f32[2,8,8,256]{3,1,2,0:T(8,128)} %bitcast.45) | data formatting | bytes 262144
  1.8 4.6 %collective-permute-start = (f32[16,8,256]{2,1,0:T(8,128)S(1)}, f32[16,8,256]{2,1,0:T(8,128)S(1)}, u32[]{:S(2)}, u32[]{:S(2)}) collective-permute-start(f32[16,8,256]{2,1,0:T(8,128)S(1)} %bitcast.46), channel_id=1, source_target_pairs={{0,7},{1,0},{2,1},{3,2},{4,3},{5,4},{6,5},{7,6},{8,15},{9,8},{10,9... | collective-permute-start | bytes 393224 | tf_op jit(solution)/shard_map/ppermute | solution.py:15
  7.0 1.1 %fusion.15 = f32[12,16,256]{2,0,1:T(8,128)S(1)} fusion(f32[16,8,256]{2,1,0:T(8,128)S(1)} %bitcast.47, s32[12]{0:T(128)} %bitcast.50, f32[12]{0:T(128)S(1)} %compare_convert_fusion), kind=kOutput, calls=%fused_computation.30 | convolution fusion | flops 4718784 | bytes 327776 | tf_op jit(solution)/shard_map/kt,bti->kbi/dot_general | solution.py:62
  8.1 0.0 copy-done
  8.1 1.7 %fusion = f32[12,16,256]{2,1,0:T(8,128)S(1)} fusion(f32[1,1,12,256,256]{4,3,2,1,0:T(8,128)S(1)} %copy-done, f32[12,16,256]{2,0,1:T(8,128)S(1)} %fusion.15), kind=kOutput, calls=%fused_computation | convolution fusion | flops 150994944 | bytes 3538944 | tf_op jit(solution)/shard_map/kbi,kij->kbj/dot_general | solution.py:63
  9.8 0.0 copy-done.3
  9.8 0.4 convolution_bitcast_fusion
  10.2 0.1 collective-permute-start.2
  10.3 0.0 collective-permute-done
  10.4 1.1 %collective-permute-start.1 = (f32[16,8,256]{2,1,0:T(8,128)S(1)}, f32[16,8,256]{2,1,0:T(8,128)S(1)}, u32[]{:S(2)}, u32[]{:S(2)}) collective-permute-start(f32[16,8,256]{2,1,0:T(8,128)S(1)} %broadcast_select_fusion.1), channel_id=1, source_target_pairs={{0,6},{1,7},{2,0},{3,1},{4,2},{5,3},{6,4},{7,5},{8,14},{9,15},{10,... | collective-permute-start | bytes 393224 | tf_op jit(solution)/shard_map/ppermute | solution.py:15
  11.4 5.2 %collective-permute-done.2 = f32[16,8,256]{2,1,0:T(8,128)} collective-permute-done((f32[16,8,256]{2,1,0:T(8,128)S(1)}, f32[16,8,256]{2,1,0:T(8,128)}, u32[]{:S(2)}, u32[]{:S(2)}) %collective-permute-start.2) | collective-permute-done | bytes 131104 | tf_op jit(solution)/shard_map/ppermute | solution.py:15
  16.7 0.1 collective-permute-start.3
  16.8 0.0 collective-permute-done.1
  16.8 0.4 fusion.8
  17.2 0.0 copy-start.1
  17.2 0.0 copy-start.2
  17.2 2.8 %fusion.2 = f32[12,16,256]{2,1,0:T(8,128)S(1)} fusion(f32[1,1,12,256,256]{4,3,2,1,0:T(8,128)S(1)} %copy-done, f32[12,16,256]{2,0,1:T(8,128)S(1)} %fusion.8), kind=kOutput, calls=%fused_computation.2 | convolution fusion | flops 150994944 | bytes 3538944 | tf_op jit(solution)/shard_map/kbj,kij->kbi/dot_general | solution.py:60
  20.0 1.1 %convolution_bitcast_fusion.1 = f32[16,8,256]{2,1,0:T(8,128)S(1)} fusion(f32[12,16,256]{2,1,0:T(8,128)S(1)} %fusion.2, s32[12]{0:T(128)} %bitcast.51, f32[12]{0:T(128)S(1)} %compare_convert_fusion), kind=kOutput, calls=%fused_computation.7 | convolution fusion | flops 4718784 | bytes 327776 | tf_op jit(solution)/shard_map/kt,kbi->bti/dot_general | solution.py:61
  21.1 2.4 %collective-permute-done.3 = f32[16,8,256]{2,1,0:T(8,128)S(1)} collective-permute-done((f32[16,8,256]{2,1,0:T(8,128)S(1)}, f32[16,8,256]{2,1,0:T(8,128)S(1)}, u32[]{:S(2)}, u32[]{:S(2)}) %collective-permute-start.3) | collective-permute-done | bytes 131104 | tf_op jit(solution)/shard_map/ppermute | solution.py:15
  23.6 11.7 %all_gather.3 = f32[4,16,2048]{2,1,0:T(8,128)} all-gather(f32[1,16,2048]{2,1,0:T(8,128)S(1)} %all_gather_reshape.3), channel_id=1, replica_groups=mesh['grp'=4,'pos'=8] {'grp'}, dimensions={0}, use_global_device_ids=true | all-gather | bytes 655360 | tf_op jit(solution)/shard_map/all_gather | solution.py:8
  35.3 1.1 %reduce_sum.9 = f32[16,2048]{1,0:T(8,128)S(1)} reduce(f32[4,16,2048]{2,1,0:T(8,128)} %all_gather.3, f32[]{:T(128)} %constant.90.clone.1), dimensions={0}, to_apply=%region_0.1 | reduce | flops 98304 | bytes 655364 | tf_op jit(solution)/shard_map/reduce_sum | solution.py:9
  36.3 0.0 copy-done.1
  36.4 0.0 copy-done.2
  36.4 0.3 convolution_bitcast_fusion.2
  36.6 14.0 %psum.14 = f32[16,16]{0,1:T(8,128)S(1)} all-reduce(f32[16,16]{0,1:T(8,128)S(1)} %convolution_bitcast_fusion.2), channel_id=1, replica_groups=mesh['grp'=4,'pos'=8] {'pos'}, use_global_device_ids=true, to_apply=%region_1.2 | all-reduce | flops 256 | bytes 2048 | tf_op jit(solution)/shard_map/psum | solution.py:69
  50.6 0.3 convolution_subtract_fusion.1
  50.9 0.7 copy.16
  51.5 1.2 %convolution_subtract_fusion = f32[16,2048]{1,0:T(8,128)S(1)} fusion(f32[16,2048]{1,0:T(8,128)S(1)} %convolution_subtract_fusion.1, f32[16,16]{1,0:T(8,128)} %param.15, f32[16,2048]{1,0:T(8,128)} %param.14), kind=kOutput, calls=%fused_computation.4 | convolution fusion | flops 6324224 | bytes 394240 | tf_op jit(solution)/shard_map/dot_general | solution.py:19
  52.7 0.2 fusion.40
  53.0 14.0 %psum.15 = f32[16,16]{0,1:T(8,128)S(1)} all-reduce(f32[16,16]{0,1:T(8,128)S(1)} %fusion.40), channel_id=1, replica_groups=mesh['grp'=4,'pos'=8] {'pos'}, use_global_device_ids=true, to_apply=%region_2.3 | all-reduce | flops 256 | bytes 2048 | tf_op jit(solution)/shard_map/psum | solution.py:71
  66.9 0.1 copy.15
  67.0 1.5 %cholesky.16 = f32[16,16]{1,0:T(8,128)S(1)} custom-call(f32[16,16]{1,0:T(8,128)S(1)} %fusion.14), custom_call_target="Cholesky" | custom-call | tf_op jit(solution)/shard_map/jit(cholesky)/cholesky | solution.py:72
  68.5 0.6 compare_reduce_fusion
  69.2 1.2 %select_bitcast_fusion = (f32[1,16,16]{2,1,0:T(8,128)S(1)}, f32[16,16]{1,0:T(8,128)}) fusion(f32[16,16]{1,0:T(8,128)S(1)} %cholesky.16, pred[]{:T(512)} %compare_reduce_fusion), kind=kLoop, calls=%fused_computation.25 | loop fusion | flops 1024 | bytes 3073 | tf_op jit(solution)/shard_map/jit(_solve_triangular)/triangular_solve | solution.py:73
  70.4 1.2 %custom-call.7 = f32[1,16,16]{1,2,0:T(8,128)S(1)} custom-call(f32[1,16,16]{2,1,0:T(8,128)S(1)} %get-tuple-element.9), custom_call_target="InvertDiagBlocksLowerTriangular" | custom-call | tf_op jit(solution)/shard_map/jit(_solve_triangular)/triangular_solve | solution.py:73
  71.6 1.0 %fusion.12 = f32[16,2048]{1,0:T(8,128)} fusion(f32[16,2048]{1,0:T(8,128)S(1)} %convolution_subtract_fusion, f32[1,16,16]{1,2,0:T(8,128)S(1)} %custom-call.7), kind=kOutput, calls=%fused_computation.21 | convolution fusion | flops 6291456 | bytes 263168 | tf_op jit(solution)/shard_map/jit(_solve_triangular)/triangular_solve | solution.py:73
  (9 shorter events, 0.1 us)
Async XLA Ops:
  0.6 7.4 %copy-start = (f32[1,1,12,256,256]{4,3,2,1,0:T(8,128)S(1)}, f32[1,1,12,256,256]{4,3,2,1,0:T(8,128)}, u32[]{:S(2)}) copy-start(f32[1,1,12,256,256]{4,3,2,1,0:T(8,128)} %param.8) | copy-start | bytes 9437188
  0.6 9.1 %copy-start.3 = (s32[1,1,12]{2,1,0:T(1,128)S(1)}, s32[1,1,12]{2,1,0:T(1,128)}, u32[]{:S(2)}) copy-start(s32[1,1,12]{2,1,0:T(1,128)} %param.10) | copy-start | bytes 148
  1.8 8.6 %collective-permute-start = (f32[16,8,256]{2,1,0:T(8,128)S(1)}, f32[16,8,256]{2,1,0:T(8,128)S(1)}, u32[]{:S(2)}, u32[]{:S(2)}) collective-permute-start(f32[16,8,256]{2,1,0:T(8,128)S(1)} %bitcast.46), channel_id=1, source_target_pairs={{0,7},{1,0},{2,1},{3,2},{4,3},{5,4},{6,5},{7,6},{8,15},{9,8},{10,9... | collective-permute-start | bytes 393224 | tf_op jit(solution)/shard_map/ppermute | solution.py:15
  10.2 6.5 %collective-permute-start.2 = (f32[16,8,256]{2,1,0:T(8,128)S(1)}, f32[16,8,256]{2,1,0:T(8,128)}, u32[]{:S(2)}, u32[]{:S(2)}) collective-permute-start(f32[16,8,256]{2,1,0:T(8,128)S(1)} %convolution_bitcast_fusion), channel_id=1, source_target_pairs={{0,1},{1,2},{2,3},{3,4},{4,5},{5,6},{6,7},{7,0},{8,9},{9,10},{10,1... | collective-permute-start | bytes 393224 | tf_op jit(solution)/shard_map/ppermute | solution.py:15
  10.4 6.4 %collective-permute-start.1 = (f32[16,8,256]{2,1,0:T(8,128)S(1)}, f32[16,8,256]{2,1,0:T(8,128)S(1)}, u32[]{:S(2)}, u32[]{:S(2)}) collective-permute-start(f32[16,8,256]{2,1,0:T(8,128)S(1)} %broadcast_select_fusion.1), channel_id=1, source_target_pairs={{0,6},{1,7},{2,0},{3,1},{4,2},{5,3},{6,4},{7,5},{8,14},{9,15},{10,... | collective-permute-start | bytes 393224 | tf_op jit(solution)/shard_map/ppermute | solution.py:15
  16.7 6.8 %collective-permute-start.3 = (f32[16,8,256]{2,1,0:T(8,128)S(1)}, f32[16,8,256]{2,1,0:T(8,128)S(1)}, u32[]{:S(2)}, u32[]{:S(2)}) collective-permute-start(f32[16,8,256]{2,1,0:T(8,128)S(1)} %broadcast_select_fusion), channel_id=1, source_target_pairs={{0,2},{1,3},{2,4},{3,5},{4,6},{5,7},{6,0},{7,1},{8,10},{9,11},{10,... | collective-permute-start | bytes 393224 | tf_op jit(solution)/shard_map/ppermute | solution.py:15
  17.2 19.1 %copy-start.1 = (f32[16,2048]{1,0:T(8,128)S(1)}, f32[16,2048]{1,0:T(8,128)}, u32[]{:S(2)}) copy-start(f32[16,2048]{1,0:T(8,128)} %param.13) | copy-start | bytes 393220
  17.2 19.1 %copy-start.2 = (f32[2048]{0:T(1024)S(1)}, f32[2048]{0:T(1024)}, u32[]{:S(2)}) copy-start(f32[2048]{0:T(1024)} %param.12) | copy-start | bytes 24580
